TPU v7x, 128 devices: a whole 4x4x4 slice. The times are simulated.
128 devices in a mesh: section: 2 (over core), dp: 64 (over y, z, x).
Axes of the slice: x: 4, y: 4, z: 4, core: 2. Of those that a mesh axis runs over, the one named last changes fastest.
Arguments:
- inputs: bfloat16 [2, 4096, 960], P(None, 'dp'), may hold values from -16 to 16
- starts: int32 [2, 4096], P(None, 'dp'), may hold values from 0 to 64, as said below
- cotangent: bfloat16 [2, 4096, 960], P(None, 'dp'), may hold values from -16 to 16
- w_query: bfloat16 [2, 960, 960], P('section', 'dp'), may hold values from -0.1875 to 0.1875
- w_key: bfloat16 [2, 960, 320], P('section', 'dp'), may hold values from -0.1875 to 0.1875
- w_value: bfloat16 [2, 960, 320], P('section', 'dp'), may hold values from -0.1875 to 0.1875
- w_output: bfloat16 [2, 960, 960], P('section', 'dp'), may hold values from -0.75 to 0.75
- w_gate: bfloat16 [2, 960, 2560], P('section', 'dp'), may hold values from -0.1875 to 0.1875
- w_up: bfloat16 [2, 960, 2560], P('section', 'dp'), may hold values from -0.1875 to 0.1875
- w_down: bfloat16 [2, 2560, 960], P('section', 'dp'), may hold values from -0.15625 to 0.15625
- attn_gain: bfloat16 [2, 960], P('section', 'dp'), may hold values from 0.25 to 1.75
- ffn_gain: bfloat16 [2, 960], P('section', 'dp'), may hold values from 0.25 to 1.75
Outputs:
- activations: bfloat16 [2, 2, 4096, 960], P('section', None, 'dp')
- input_grads: bfloat16 [2, 2, 4096, 960], P('section', None, 'dp')
- grad_query: float32 [2, 960, 960], P('section', 'dp')
- grad_key: float32 [2, 960, 320], P('section', 'dp')
- grad_value: float32 [2, 960, 320], P('section', 'dp')
- grad_output: float32 [2, 960, 960], P('section', 'dp')
- grad_gate: float32 [2, 960, 2560], P('section', 'dp')
- grad_up: float32 [2, 960, 2560], P('section', 'dp')
- grad_down: float32 [2, 2560, 960], P('section', 'dp')
- grad_attn_gain: float32 [2, 960], P('section', 'dp')
- grad_ffn_gain: float32 [2, 960], P('section', 'dp')
Inputs may be any that keep to these rules, and one draw needn't show every extreme that they name: `starts`: within each aligned block of 64 rows (one index of dp, one micro-batch) sequences lie end to end from the block's first row, each row holding the block-local index of its sequence's first row; the rows after the last sequence are padding and hold 64. At least a quarter of every block's rows are in sequences, and some blocks are full.
All inputs are finite; a program needn't handle non-finite values.
Results may differ from a plain program's by a relative error of at most 0.023.
Values may be sent and summed in bfloat16 or wider, within the bound.
No kernel may reach another device: no remote copies, remote signals or barrier semaphores. Data moves between devices by JAX's collectives and lax.ppermute only.
A program may use at most 256 MiB of HBM per device.

v0:
```python
import jax
import jax.numpy as jnp
from jax import lax
from jax.sharding import PartitionSpec as P

D = 960
HEADS = 15
KV_HEADS = 5
GROUP = HEADS // KV_HEADS
HEAD_DIM = 64
FF = 2560
QD = 960
KVD = 320
OWNERS = 64
SLOT = 15
PADDED = 16
DOWN_ROWS = 40
norm_eps = 1e-05
masked_score = -1e30
rope_base = 10000.0
f32 = jnp.float32
bf16 = jnp.bfloat16


def gray(value):
    return value ^ value >> 1


AXIS_SHIFT = {"y": 4, "z": 2, "x": 0}
BITS = (("y", 1), ("y", 0), ("z", 1), ("z", 0), ("x", 1), ("x", 0))


def partner_pairs(bit):
    axis, place = bit
    shift = AXIS_SHIFT[axis]
    pairs = []
    for source in range(OWNERS):
        coordinate = source >> shift & 3
        other = gray(gray(coordinate) ^ 1 << place)
        pairs.append((source, source + (other - coordinate << shift)))
    return pairs


def owner_of(position):
    me = lax.axis_index("dp")
    owner = 0
    for shift in (4, 2, 0):
        owner = owner + (gray(gray(me >> shift & 3) ^ position >> shift & 3) << shift)
    return owner


def dot(left, right):
    return jnp.dot(left, right, preferred_element_type=f32)


def dot_t(left, right):
    return lax.dot_general(left, right, (((1,), (1,)), ((), ())), preferred_element_type=f32)


def spread_matrix():
    row = lax.broadcasted_iota(jnp.int32, (D, OWNERS * PADDED), 0)
    col = lax.broadcasted_iota(jnp.int32, (D, OWNERS * PADDED), 1)
    return ((row == SLOT * (col // PADDED) + col % PADDED) & (col % PADDED < SLOT)).astype(bf16)


def own_spread():
    row = lax.broadcasted_iota(jnp.int32, (OWNERS * PADDED, D), 0)
    col = lax.broadcasted_iota(jnp.int32, (OWNERS * PADDED, D), 1)
    owner = owner_of(row // PADDED)
    return ((col == SLOT * owner + row % PADDED) & (row % PADDED < SLOT)).astype(bf16)


def gather_rows(values, spread):
    high = values.astype(bf16)
    low = (values - high.astype(f32)).astype(bf16)
    return dot_t(high, spread) + dot_t(low, spread)


def geometry(starts):
    rows = starts.shape[-1]
    local = jnp.arange(rows, dtype=jnp.int32)
    live = starts <= local
    position = jnp.where(live, local - starts, 0).astype(f32)
    frequency = rope_base ** (-2.0 * jnp.arange(HEAD_DIM // 2, dtype=f32) / HEAD_DIM)
    angles = position[..., None, None] * frequency
    causal = local[None, :] <= local[:, None]
    inside = local >= starts[..., None]
    diagonal = local[None, :] == local[:, None]
    allowed = causal & inside | diagonal
    return (live.astype(f32).reshape(-1, 1), jnp.cos(angles), jnp.sin(angles), allowed)


def rotate(values, cosine, sine):
    half = HEAD_DIM // 2
    first, second = (values[..., :half], values[..., half:])
    return jnp.concatenate(
        [first * cosine - second * sine, second * cosine + first * sine], axis=-1
    )


def norm_parts(values):
    inverse = lax.rsqrt(jnp.mean(values * values, axis=-1, keepdims=True) + norm_eps)
    return (values * inverse, inverse)


def norm_back(grad, normal, inverse, gain):
    scaled = grad * gain
    return inverse * (scaled - normal * jnp.mean(scaled * normal, axis=-1, keepdims=True))


def forward(source, weights, geo, spread):
    w_query, w_key, w_value, w_output, w_gate, w_up, w_down, attn_gain, ffn_gain = weights
    live, cosine, sine, allowed = geo
    micro, rows = cosine.shape[:2]
    h = source.astype(f32)
    n1, r1 = norm_parts(h)
    a = (n1 * attn_gain).astype(bf16)
    a_wide = dot(a, spread).astype(bf16)
    q = rotate(dot(a_wide, w_query).reshape(micro, rows, HEADS, HEAD_DIM), cosine, sine)
    k = rotate(dot(a_wide, w_key).reshape(micro, rows, KV_HEADS, HEAD_DIM), cosine, sine)
    v = dot(a_wide, w_value).astype(bf16).reshape(micro, rows, KV_HEADS, HEAD_DIM)
    q = q.astype(bf16).reshape(micro, rows, KV_HEADS, GROUP, HEAD_DIM)
    k = k.astype(bf16)
    s = jnp.einsum("bqhgd,bkhd->bhgqk", q, k, preferred_element_type=f32) * HEAD_DIM ** (-0.5)
    s = jnp.where(allowed[:, None, None], s, masked_score)
    e = jnp.exp(s - jnp.max(s, axis=-1, keepdims=True))
    p = e / jnp.sum(e, axis=-1, keepdims=True)
    p_low = p.astype(bf16)
    o = jnp.einsum("bhgqk,bkhd->bqhgd", p_low, v, preferred_element_type=f32)
    o = o.reshape(micro * rows, QD).astype(bf16)
    m = h + dot(dot(o, spread).astype(bf16), w_output)
    n2, r2 = norm_parts(m)
    b = (n2 * ffn_gain).astype(bf16)
    b_wide = dot(b, spread).astype(bf16)
    gate = dot(b_wide, w_gate)
    up = dot(b_wide, w_up)
    hidden = (gate * jax.nn.sigmoid(gate) * up).astype(bf16)
    result = ((m + dot(hidden, w_down)) * live).astype(bf16)
    return (result, (n1, r1, a, q, k, v, p, p_low, o, n2, r2, b, gate, up, hidden))


def backward(saved, upstream, weights, geo, spread):
    w_query, w_key, w_value, w_output, w_gate, w_up, w_down, attn_gain, ffn_gain = weights
    n1, r1, a, q, k, v, p, p_low, o, n2, r2, b, gate, up, hidden = saved
    live, cosine, sine, allowed = geo
    micro, rows = cosine.shape[:2]
    d3 = upstream.astype(f32) * live
    d3_low = d3.astype(bf16)
    dhidden = dot_t(d3_low, w_down)
    sig = jax.nn.sigmoid(gate)
    dg = (dhidden * up * sig * (1.0 + gate * (1.0 - sig))).astype(bf16)
    du = (dhidden * gate * sig).astype(bf16)
    db = gather_rows(dot_t(dg, w_gate) + dot_t(du, w_up), spread)
    dm = d3 + norm_back(db, n2, r2, ffn_gain)
    dffn = jnp.sum(db * n2, axis=0)
    dm_low = dm.astype(bf16)
    do = dot_t(dot_t(dm_low, w_output).astype(bf16), spread).astype(bf16)
    do = do.reshape(micro, rows, KV_HEADS, GROUP, HEAD_DIM)
    dp = jnp.einsum("bqhgd,bkhd->bhgqk", do, v, preferred_element_type=f32)
    dv = jnp.einsum("bhgqk,bqhgd->bkhd", p_low, do, preferred_element_type=f32)
    ds = (p * (dp - jnp.sum(p * dp, axis=-1, keepdims=True))).astype(bf16)
    dq = jnp.einsum("bhgqk,bkhd->bqhgd", ds, k, preferred_element_type=f32) * HEAD_DIM ** (-0.5)
    dk = jnp.einsum("bhgqk,bqhgd->bkhd", ds, q, preferred_element_type=f32) * HEAD_DIM ** (-0.5)
    dq = rotate(dq.reshape(micro, rows, HEADS, HEAD_DIM), cosine, -sine)
    dq = dq.reshape(micro * rows, QD).astype(bf16)
    dk = rotate(dk, cosine, -sine).reshape(micro * rows, KVD).astype(bf16)
    dv = dv.reshape(micro * rows, KVD).astype(bf16)
    da = gather_rows(dot_t(dq, w_query) + dot_t(dk, w_key) + dot_t(dv, w_value), spread)
    dh = dm + norm_back(da, n1, r1, attn_gain)
    dattn = jnp.sum(da * n1, axis=0)
    return (dh.astype(bf16), (d3_low, dg, du, dm_low, dq, dk, dv, dattn, dffn))


def blocks(left_t, rows):
    return left_t.reshape((2,) * 6 + (rows, left_t.shape[-1]))


def pick(array, dim, index):
    return lax.index_in_dim(array, index, dim, keepdims=False)


def product(left_t, right):
    flat = left_t.reshape(-1, left_t.shape[-1])
    return dot(flat, right).reshape(left_t.shape[:-1] + (right.shape[-1],))


def first_halves(left_t, right, order, extra=None):
    dim = BITS.index(order[0])
    halves = []
    for index in (1, 0):
        value = product(pick(left_t, dim, index), right)
        if extra is not None:
            value = value + pick(extra, dim, index)
        halves.append(value.astype(bf16))
    return (halves[1], halves[0])


def rotations(place, then):
    axes = "yzx"
    result = []
    for turn in range(3):
        turned = axes[turn:] + axes[:turn]
        result.append(
            tuple(((axis, place) for axis in turned)) + tuple(((axis, then) for axis in turned))
        )
    return result


ORDERS = (rotations(1, 0), rotations(0, 1))


def halving(kept, sent, order, left, last):
    bit = order[0]
    left = [other for other in left if other != bit]
    arrived = lax.ppermute(sent, "dp", partner_pairs(bit))
    if len(order) == 1:
        return (kept.astype(f32) + arrived.astype(f32), None, left)
    if last:
        return ((kept.astype(f32) + arrived.astype(f32)).astype(bf16), None, left)
    dim = left.index(order[1])
    next_sent = pick(kept, dim, 1).astype(f32) + pick(arrived, dim, 1).astype(f32)
    next_kept = pick(kept, dim, 0).astype(f32) + pick(arrived, dim, 0).astype(f32)
    return (next_kept.astype(bf16), next_sent.astype(bf16), left)


def reduce_three(members, orders):
    after = []
    for (left_t, right, extra), order in zip(members, orders):
        kept, sent = first_halves(left_t, right, order, extra)
        left = list(BITS)
        for step in range(3):
            kept, sent, left = halving(kept, sent, order[step:], left, step == 2)
        after.append(kept)
    return (after, left)


def finish(value, left, order):
    dim = left.index(order[0])
    kept, sent = (pick(value, dim, 0), pick(value, dim, 1))
    for step in range(3):
        kept, sent, left = halving(kept, sent, order[step:], left, False)
    return kept


def xor_order(left_t):
    width = left_t.shape[-1]
    value = left_t.reshape(4, 4, 4, DOWN_ROWS, width)
    me = lax.axis_index("dp")
    for dim, shift in enumerate((4, 2, 0)):
        mine = gray(me >> shift & 3)
        value = jnp.concatenate(
            [lax.dynamic_slice_in_dim(value, gray(mine ^ place), 1, dim) for place in range(4)],
            axis=dim,
        )
    return value


def body(
    inputs,
    starts,
    cotangent,
    w_query,
    w_key,
    w_value,
    w_output,
    w_gate,
    w_up,
    w_down,
    attn_gain,
    ffn_gain,
):
    section = lax.axis_index("section")
    micro, rows = starts.shape
    gains = jnp.concatenate([attn_gain, ffn_gain], axis=1)
    gain_row = jnp.pad(gains, ((0, 0), (0, D - gains.shape[1])))
    blank = jnp.zeros((1, D), bf16)
    slabs = (
        w_query[0],
        w_output[0],
        w_gate[0, :, :960],
        w_gate[0, :, 960:1920],
        w_up[0, :, :960],
        w_up[0, :, 960:1920],
        jnp.concatenate([w_gate[0, :, 1920:], w_key[0]], axis=1),
        jnp.concatenate([w_up[0, :, 1920:], w_value[0]], axis=1),
    )
    pieces = []
    for index, slab in enumerate(slabs):
        pieces += [slab, gain_row if index == 0 else blank]
    packed = jnp.concatenate(pieces + [w_down[0]], axis=0)[None]
    everything = lax.all_gather(packed, "dp", axis=0, tiled=True)

    def slab_of(index):
        part = everything[:, PADDED * index : PADDED * (index + 1)]
        return part.reshape(OWNERS * PADDED, D)

    mixed_gate, mixed_up = (slab_of(6), slab_of(7))
    all_gains = everything[:, SLOT, : 2 * SLOT].astype(f32)
    weights = (
        slab_of(0),
        mixed_gate[:, 640:],
        mixed_up[:, 640:],
        slab_of(1),
        jnp.concatenate([slab_of(2), slab_of(3), mixed_gate[:, :640]], axis=1),
        jnp.concatenate([slab_of(4), slab_of(5), mixed_up[:, :640]], axis=1),
        everything[:, 8 * PADDED :].reshape(FF, D),
        all_gains[:, :SLOT].reshape(D),
        all_gains[:, SLOT:].reshape(D),
    )
    spread = spread_matrix()
    mine = own_spread()
    geo = geometry(starts)
    first_in = inputs.reshape(micro * rows, D)
    top = cotangent.reshape(micro * rows, D)
    made, _ = forward(first_in, weights, geo, spread)
    arrived = lax.ppermute(made, "section", [(0, 1)])
    source = jnp.where(section == 0, first_in, arrived)
    result, saved = forward(source, weights, geo, spread)
    back, _ = backward(saved, top, weights, geo, spread)
    returned = lax.ppermute(back, "section", [(1, 0)])
    upstream = jnp.where(section == 1, top, returned)
    grad_rows, grads = backward(saved, upstream, weights, geo, spread)
    d3_low, dg, du, dm_low, dq, dk, dv, dattn, dffn = grads
    a, o, b, hidden = (saved[2], saved[8], saved[11], saved[14])
    a_t = blocks(dot_t(mine, a).astype(bf16), PADDED)
    o_t = blocks(dot_t(mine, o).astype(bf16), PADDED)
    b_t = blocks(dot_t(mine, b).astype(bf16), PADDED)
    hidden_t = blocks(xor_order(hidden.T), DOWN_ROWS)
    half = FF // 2
    outs = []
    for group, orders in enumerate(ORDERS):
        cut = slice(group * half, (group + 1) * half)
        down_cut = slice(0, 512) if group == 0 else slice(512, D)
        members = (
            (b_t, dg[:, cut], None),
            (b_t, du[:, cut], None),
            (hidden_t, d3_low[:, down_cut], None),
        )
        (gate_part, up_part, down_part), left = reduce_three(members, orders)
        pair = jnp.concatenate([gate_part, up_part], axis=-1)
        outs.append((finish(pair, left, orders[0][3:]), finish(down_part, left, orders[1][3:])))
    grad_gate = jnp.concatenate([outs[0][0][:SLOT, :half], outs[1][0][:SLOT, :half]], axis=1)
    grad_up = jnp.concatenate([outs[0][0][:SLOT, half:], outs[1][0][:SLOT, half:]], axis=1)
    grad_down = jnp.concatenate([outs[0][1], outs[1][1]], axis=1)
    owner = owner_of(jnp.arange(OWNERS, dtype=jnp.int32))
    choose = (owner[:, None] == jnp.arange(OWNERS, dtype=jnp.int32)[None, :]).astype(f32)
    both = jnp.concatenate([dattn.reshape(OWNERS, SLOT), dffn.reshape(OWNERS, SLOT)], axis=1)
    both = jnp.dot(choose, both, precision=lax.Precision.HIGHEST)
    extra = jnp.pad(both[:, None, :], ((0, 0), (SLOT, 0), (0, 512 - 2 * SLOT)))
    extra = extra.reshape((2,) * 6 + extra.shape[1:])
    dqkv = jnp.concatenate([dq, dk, dv], axis=1)
    cuts = (((0, 512), (512, 896), (0, 512)), ((896, 1280), (1280, 1600), (512, 960)))
    ends = []
    for group, orders in enumerate(ORDERS):
        (lo0, hi0), (lo1, hi1), (lo2, hi2) = cuts[group]
        members = (
            (a_t, dqkv[:, lo0:hi0], extra if group == 0 else None),
            (a_t, dqkv[:, lo1:hi1], None),
            (o_t, dm_low[:, lo2:hi2], None),
        )
        parts, left = reduce_three(members, orders)
        ends.append(finish(jnp.concatenate(parts, axis=-1), left, orders[2][3:]))
    dqkv_sum = jnp.concatenate([ends[0][:, :896], ends[1][:, :704]], axis=1)
    grad_output = jnp.concatenate([ends[0][:SLOT, 896:], ends[1][:SLOT, 704:]], axis=1)
    gain_sum = dqkv_sum[SLOT]
    return (
        result.reshape(1, micro, rows, D),
        grad_rows.reshape(1, micro, rows, D),
        dqkv_sum[None, :SLOT, :QD],
        dqkv_sum[None, :SLOT, QD : QD + KVD],
        dqkv_sum[None, :SLOT, QD + KVD :],
        grad_output[None],
        grad_gate[None],
        grad_up[None],
        grad_down[None],
        gain_sum[None, :SLOT],
        gain_sum[None, SLOT : 2 * SLOT],
    )


def solution(mesh):
    split = P("section", "dp", None)
    return jax.shard_map(
        body,
        mesh=mesh,
        in_specs=(P(None, "dp", None), P(None, "dp"), P(None, "dp", None))
        + (split,) * 7
        + (P("section", "dp"),) * 2,
        out_specs=(P("section", None, "dp", None),) * 2 + (split,) * 7 + (P("section", "dp"),) * 2,
        check_vma=False,
    )
```

profile of v0, /device:TPU:0, one launch (start us, length us, event | category | flops | bytes accessed | tf_op | source)
XLA Modules:
  0.0 695.9 jit_solution(18312639597677706957)
XLA Ops:
  11.1 18.6 %concatenate.104 = bf16[168,960]{1,0:T(8,128)(2,1)} concatenate(bf16[15,960]{1,0:T(8,128)(2,1)} %bitcast.888, bf16[1,960]{1,0:T(2,128)(2,1)S(1)} %fusion.272, bf16[15,960]{1,0:T(8,128)(2,1)} %bitcast.889, bf16[1,960]{1,0:T(2,128)(2,1)S(1)} %broadcast.365, bf16[15,960]{1,0:T(8,128)(2,1)S(1)} %get-tuple-element.178, bf16[1,960]{1,0:T(2,128)(2,1)S(1)} %broadcast.365, ...), dimensions={0} | concatenate | bytes 645120 | tf_op jit(solution)/shard_map/concatenate | solution.py:290
  40.9 112.3 %all-gather.3.cloned.1.call-done = bf16[10752,960]{1,0:T(8,128)(2,1)} async-done(((bf16[168,960]{1,0:T(8,128)(2,1)}), bf16[10752,960]{1,0:T(8,128)(2,1)}) %all-gather.3.cloned.1.call-update) | async-done | bytes 20643856 | tf_op jit(solution)/shard_map/all_gather | solution.py:291
  154.1 5.5 slice.1024
  159.6 11.7 %fusion.328 = (bf16[64,16,960]{2,1,0:T(8,128)(2,1)}, bf16[64,16,960]{2,1,0:T(8,128)(2,1)}, bf16[64,16,960]{2,1,0:T(8,128)(2,1)}, bf16[64,16,960]{2,1,0:T(8,128)(...) fusion(bf16[64,168,960]{2,1,0:T(8,128)(2,1)} %bitcast.821), kind=kLoop, calls=%fused_computation.648 | loop fusion | bytes 31457280 | tf_op jit(solution)/shard_map/slice | solution.py:294
  211.4 4.6 multiply_reduce_fusion.7
  217.2 9.6 %concatenate.109 = bf16[1024,2560]{1,0:T(8,128)(2,1)} concatenate(bf16[1024,960]{1,0:T(8,128)(2,1)} %bitcast.847, bf16[1024,960]{1,0:T(8,128)(2,1)} %bitcast.846, bf16[1024,640]{1,0:T(8,128)(2,1)} %slice.1020), dimensions={1} | concatenate | bytes 10485760 | tf_op jit(solution)/shard_map/concatenate | solution.py:304
  231.4 9.6 %concatenate.110 = bf16[1024,2560]{1,0:T(8,128)(2,1)} concatenate(bf16[1024,960]{1,0:T(8,128)(2,1)} %bitcast.845, bf16[1024,960]{1,0:T(8,128)(2,1)} %bitcast.844, bf16[1024,640]{1,0:T(8,128)(2,1)S(1)} %slice.1023), dimensions={1} | concatenate | bytes 10485760 | tf_op jit(solution)/shard_map/concatenate | solution.py:305
  241.0 7.0 %fusion.42 = bf16[128,960]{0,1:T(8,128)(2,1)S(1)} fusion(f32[128,960]{0,1:T(8,128)} %get-tuple-element.159, bf16[2560,960]{1,0:T(8,128)(2,1)} %bitcast.822, bf16[128,1024]{1,0:T(8,128)(2,1)} %copy-done.67, bf16[1024,2560]{1,0:T(8,128)(2,1)} %concatenate.110, f32[128,2560]{1,0:T(8,128)} %fusion.346, f32[128]{0:T(128)S(1)} %mul.607), kind=kOutput, calls=%fused_computation.134 | convolution fusion | flops 1302568960 | bytes 12468736 | tf_op jit(solution)/shard_map/dot_general | solution.py:53
  249.9 5.4 fusion.349
  281.1 4.1 convolution_convert_fusion.25
  307.5 4.1 convolution_convert_fusion.36
  353.7 3.7 convolution_convert_fusion.35
  431.8 4.3 pad_slice_fusion.1
  436.1 3.7 copy.174
  457.9 24.5 %collective-permute-done.18 = bf16[2,2,2,2,16,320]{5,4,2,3,0,1:T(8,128)(2,1)S(1)} collective-permute-done((bf16[2,2,2,2,16,320]{5,4,2,3,0,1:T(8,128)(2,1)S(1)}, bf16[2,2,2,2,16,320]{5,4,2,3,0,1:T(8,128)(2,1)S(1)}, u32[]{:S(2)}, u32[]{:S(2)}) %collective-permute-start.18) | collective-permute-done | bytes 163872 | tf_op jit(solution)/shard_map/ppermute | solution.py:215
  488.4 3.9 collective-permute-done.19
  501.7 19.8 %collective-permute-done.7 = bf16[2,2,2,16,384]{4,3,2,1,0:T(8,128)(2,1)S(1)} collective-permute-done((bf16[2,2,2,16,384]{4,3,2,1,0:T(8,128)(2,1)S(1)}, bf16[2,2,2,16,384]{4,3,2,1,0:T(8,128)(2,1)S(1)}, u32[]{:S(2)}, u32[]{:S(2)}) %collective-permute-start.7) | collective-permute-done | bytes 98336 | tf_op jit(solution)/shard_map/ppermute | solution.py:215
  529.2 4.4 collective-permute-done.3
  534.7 3.9 collective-permute-done.22
  541.7 3.6 collective-permute-done.10
  559.7 4.1 collective-permute-done.24
  569.1 5.5 collective-permute-done.11
  576.2 4.1 collective-permute-done.12
  596.1 13.1 %collective-permute-done.29 = bf16[2,2,2,2,2,16,1280]{6,5,4,2,1,3,0:T(8,128)(2,1)S(1)} collective-permute-done((bf16[2,2,2,2,2,16,1280]{6,5,4,2,1,3,0:T(8,128)(2,1)S(1)}, bf16[2,2,2,2,2,16,1280]{6,5,4,2,1,3,0:T(8,128)(2,1)S(1)}, u32[]{:S(2)}, u32[]{:S(2)}) %collective-permute-start.29) | collective-permute-done | bytes 1310752 | tf_op jit(solution)/shard_map/ppermute | solution.py:215
  609.6 4.2 collective-permute-done.38
  621.4 3.8 collective-permute-done.52
  628.9 5.2 collective-permute-done.53
  636.9 4.4 collective-permute-done.54
  644.7 8.8 %collective-permute-done.55 = bf16[40,448]{1,0:T(8,128)(2,1)S(1)} collective-permute-done((bf16[40,448]{1,0:T(8,128)(2,1)S(1)}, bf16[40,448]{1,0:T(8,128)(2,1)S(1)}, u32[]{:S(2)}, u32[]{:S(2)}) %collective-permute-start.55) | collective-permute-done | bytes 35872 | tf_op jit(solution)/shard_map/ppermute | solution.py:215
  669.2 5.2 collective-permute-done.41
  675.5 5.6 collective-permute-done.42
  682.5 4.4 collective-permute-done.43
  (625 shorter events, 346.3 us)
Async XLA Ops:
  7.2 146.0 %all-gather.3.cloned.1.call-start = ((), (), s32[]{:S(2)}) async-start(), calls=%async_computation | async-start | bytes 22364160 | tf_op jit(solution)/shard_map/all_gather | solution.py:291
  248.1 7.3 %collective-permute-start = (bf16[128,960]{0,1:T(8,128)(2,1)S(1)}, bf16[128,960]{0,1:T(8,128)(2,1)S(1)}, u32[]{:S(2)}, u32[]{:S(2)}) collective-permute-start(bf16[128,960]{0,1:T(8,128)(2,1)S(1)} %fusion.42), channel_id=1, source_target_pairs={{0,64},{1,65},{2,66},{3,67},{4,68},{5,69},{6,70},{7,71},{8,72},{9,... | collective-permute-start | bytes 737288 | tf_op jit(solution)/shard_map/ppermute | solution.py:316
  398.7 54.5 %collective-permute-start.5 = (bf16[2,2,2,2,2,16,384]{6,5,4,2,1,3,0:T(8,128)(2,1)}, bf16[2,2,2,2,2,16,384]{6,5,4,2,1,3,0:T(8,128)(2,1)}, u32[]{:S(2)}, u32[]{:S(2)}) collective-permute-start(bf16[2,2,2,2,2,16,384]{6,5,4,2,1,3,0:T(8,128)(2,1)} %convolution_convert_fusion.22), channel_id=1, source_target_pairs={{0,12},{1,13},{2,14},{3,15},{4,8},{5,9},{6,10},{7,11},{8,4},{9,5},... | collective-permute-start | bytes 1179656 | tf_op jit(solution)/shard_map/ppermute | solution.py:215
  401.5 48.7 %collective-permute-start.14 = (bf16[2,2,2,2,2,16,384]{6,5,1,3,0,4,2:T(8,128)(2,1)}, bf16[2,2,2,2,2,16,384]{6,5,1,3,0,4,2:T(8,128)(2,1)}, u32[]{:S(2)}, u32[]{:S(2)}) collective-permute-start(bf16[2,2,2,2,2,16,384]{6,5,1,3,0,4,2:T(8,128)(2,1)} %convolution_convert_fusion.20), channel_id=1, source_target_pairs={{0,16},{1,17},{2,18},{3,19},{4,20},{5,21},{6,22},{7,23},{8,24},{9,... | collective-permute-start | bytes 1179656 | tf_op jit(solution)/shard_map/ppermute | solution.py:215
  404.0 43.2 %collective-permute-start.17 = (bf16[2,2,2,2,2,16,320]{6,5,2,3,0,1,4:T(8,128)(2,1)}, bf16[2,2,2,2,2,16,320]{6,5,2,3,0,1,4:T(8,128)(2,1)}, u32[]{:S(2)}, u32[]{:S(2)}) collective-permute-start(bf16[2,2,2,2,2,16,320]{6,5,2,3,0,1,4:T(8,128)(2,1)} %convolution_convert_fusion.18), channel_id=1, source_target_pairs={{0,4},{1,5},{2,6},{3,7},{4,0},{5,1},{6,2},{7,3},{8,12},{9,13},{10,... | collective-permute-start | bytes 983048 | tf_op jit(solution)/shard_map/ppermute | solution.py:215
  411.2 73.0 %collective-permute-start.8 = (bf16[2,2,2,2,2,16,512]{6,5,4,3,1,2,0:T(8,128)(2,1)}, bf16[2,2,2,2,2,16,512]{6,5,4,3,1,2,0:T(8,128)(2,1)}, u32[]{:S(2)}, u32[]{:S(2)}) collective-permute-start(bf16[2,2,2,2,2,16,512]{6,5,4,3,1,2,0:T(8,128)(2,1)} %convolution_convert_fusion.14), channel_id=1, source_target_pairs={{0,3},{1,2},{2,1},{3,0},{4,7},{5,6},{6,5},{7,4},{8,11},{9,10},{10,... | collective-permute-start | bytes 1572872 | tf_op jit(solution)/shard_map/ppermute | solution.py:215
  412.7 43.9 %collective-permute-start.20 = (bf16[2,2,2,2,2,16,448]{6,5,2,4,0,3,1:T(8,128)(2,1)}, bf16[2,2,2,2,2,16,448]{6,5,2,4,0,3,1:T(8,128)(2,1)}, u32[]{:S(2)}, u32[]{:S(2)}) collective-permute-start(bf16[2,2,2,2,2,16,448]{6,5,2,4,0,3,1:T(8,128)(2,1)} %convolution_convert_fusion.12), channel_id=1, source_target_pairs={{0,1},{1,0},{2,3},{3,2},{4,5},{5,4},{6,7},{7,6},{8,9},{9,8},{10,11... | collective-permute-start | bytes 1376264 | tf_op jit(solution)/shard_map/ppermute | solution.py:215
  447.3 134.9 %collective-permute-start.50 = (bf16[2,2,2,2,2,40,448]{6,5,4,0,2,3,1:T(8,128)(2,1)}, bf16[2,2,2,2,2,40,448]{6,5,4,0,2,3,1:T(8,128)(2,1)}, u32[]{:S(2)}, u32[]{:S(2)}) collective-permute-start(bf16[2,2,2,2,2,40,448]{6,5,4,0,2,3,1:T(8,128)(2,1)} %convolution_convert_fusion.8), channel_id=1, source_target_pairs={{0,1},{1,0},{2,3},{3,2},{4,5},{5,4},{6,7},{7,6},{8,9},{9,8},{10,11... | collective-permute-start | bytes 3440648 | tf_op jit(solution)/shard_map/ppermute | solution.py:215
  450.3 138.6 %collective-permute-start.44 = (bf16[2,2,2,2,2,40,512]{6,5,4,3,1,2,0:T(8,128)(2,1)}, bf16[2,2,2,2,2,40,512]{6,5,4,3,1,2,0:T(8,128)(2,1)}, u32[]{:S(2)}, u32[]{:S(2)}) collective-permute-start(bf16[2,2,2,2,2,40,512]{6,5,4,3,1,2,0:T(8,128)(2,1)} %convolution_convert_fusion.10), channel_id=1, source_target_pairs={{0,3},{1,2},{2,1},{3,0},{4,7},{5,6},{6,5},{7,4},{8,11},{9,10},{10,... | collective-permute-start | bytes 3932168 | tf_op jit(solution)/shard_map/ppermute | solution.py:215
  453.2 34.3 %collective-permute-start.2 = (bf16[2,2,2,2,2,16,512]{6,5,4,2,0,3,1:T(8,128)(2,1)S(1)}, bf16[2,2,2,2,2,16,512]{6,5,4,2,0,3,1:T(8,128)(2,1)S(1)}, u32[]{:S(2)}, u32[]{:S(2)}) collective-permute-start(bf16[2,2,2,2,2,16,512]{6,5,4,2,0,3,1:T(8,128)(2,1)S(1)} %fusion.34), channel_id=1, source_target_pairs={{0,48},{1,49},{2,50},{3,51},{4,52},{5,53},{6,54},{7,55},{8,56},{9,... | collective-permute-start | bytes 1572872 | tf_op jit(solution)/shard_map/ppermute | solution.py:215
  456.5 25.9 %collective-permute-start.18 = (bf16[2,2,2,2,16,320]{5,4,2,3,0,1:T(8,128)(2,1)S(1)}, bf16[2,2,2,2,16,320]{5,4,2,3,0,1:T(8,128)(2,1)S(1)}, u32[]{:S(2)}, u32[]{:S(2)}) collective-permute-start(bf16[2,2,2,2,16,320]{5,4,2,3,0,1:T(8,128)(2,1)S(1)} %get-tuple-element.78), channel_id=1, source_target_pairs={{0,1},{1,0},{2,3},{3,2},{4,5},{5,4},{6,7},{7,6},{8,9},{9,8},{10,11... | collective-permute-start | bytes 491528 | tf_op jit(solution)/shard_map/ppermute | solution.py:215
  482.4 107.9 %collective-permute-start.26 = (bf16[2,2,2,2,2,16,1280]{6,5,4,2,0,3,1:T(8,128)(2,1)}, bf16[2,2,2,2,2,16,1280]{6,5,4,2,0,3,1:T(8,128)(2,1)}, u32[]{:S(2)}, u32[]{:S(2)}) collective-permute-start(bf16[2,2,2,2,2,16,1280]{6,5,4,2,0,3,1:T(8,128)(2,1)} %convolution_convert_fusion.6), channel_id=1, source_target_pairs={{0,48},{1,49},{2,50},{3,51},{4,52},{5,53},{6,54},{7,55},{8,56},{9,... | collective-permute-start | bytes 3932168 | tf_op jit(solution)/shard_map/ppermute | solution.py:215
  484.2 9.9 %collective-permute-start.6 = (bf16[2,2,2,2,16,384]{5,4,3,2,1,0:T(8,128)(2,1)S(1)}, bf16[2,2,2,2,16,384]{5,4,3,2,1,0:T(8,128)(2,1)S(1)}, u32[]{:S(2)}, u32[]{:S(2)}) collective-permute-start(bf16[2,2,2,2,16,384]{5,4,3,2,1,0:T(8,128)(2,1)S(1)} %get-tuple-element.76), channel_id=1, source_target_pairs={{0,3},{1,2},{2,1},{3,0},{4,7},{5,6},{6,5},{7,4},{8,11},{9,10},{10,... | collective-permute-start | bytes 589832 | tf_op jit(solution)/shard_map/ppermute | solution.py:215
  497.9 30.6 %collective-permute-start.9 = (bf16[2,2,2,2,16,512]{5,4,3,2,0,1:T(8,128)(2,1)S(1)}, bf16[2,2,2,2,16,512]{5,4,3,2,0,1:T(8,128)(2,1)S(1)}, u32[]{:S(2)}, u32[]{:S(2)}) collective-permute-start(bf16[2,2,2,2,16,512]{5,4,3,2,0,1:T(8,128)(2,1)S(1)} %get-tuple-element.60), channel_id=1, source_target_pairs={{0,48},{1,49},{2,50},{3,51},{4,52},{5,53},{6,54},{7,55},{8,56},{9,... | collective-permute-start | bytes 786440 | tf_op jit(solution)/shard_map/ppermute | solution.py:215
  500.5 20.9 %collective-permute-start.7 = (bf16[2,2,2,16,384]{4,3,2,1,0:T(8,128)(2,1)S(1)}, bf16[2,2,2,16,384]{4,3,2,1,0:T(8,128)(2,1)S(1)}, u32[]{:S(2)}, u32[]{:S(2)}) collective-permute-start(bf16[2,2,2,16,384]{4,3,2,1,0:T(8,128)(2,1)S(1)} %fusion.229), channel_id=1, source_target_pairs={{0,48},{1,49},{2,50},{3,51},{4,52},{5,53},{6,54},{7,55},{8,56},{9,... | collective-permute-start | bytes 294920 | tf_op jit(solution)/shard_map/ppermute | solution.py:215
  526.1 7.6 %collective-permute-start.3 = (bf16[2,2,2,2,16,512]{5,4,3,2,1,0:T(8,128)(2,1)S(1)}, bf16[2,2,2,2,16,512]{5,4,3,2,1,0:T(8,128)(2,1)S(1)}, u32[]{:S(2)}, u32[]{:S(2)}) collective-permute-start(bf16[2,2,2,2,16,512]{5,4,3,2,1,0:T(8,128)(2,1)S(1)} %fusion.147), channel_id=1, source_target_pairs={{0,12},{1,13},{2,14},{3,15},{4,8},{5,9},{6,10},{7,11},{8,4},{9,5},... | collective-permute-start | bytes 786440 | tf_op jit(solution)/shard_map/ppermute | solution.py:215
  528.5 65.3 %collective-permute-start.35 = (bf16[2,2,2,2,2,16,1280]{6,5,3,1,0,4,2:T(8,128)(2,1)}, bf16[2,2,2,2,2,16,1280]{6,5,3,1,0,4,2:T(8,128)(2,1)}, u32[]{:S(2)}, u32[]{:S(2)}) collective-permute-start(bf16[2,2,2,2,2,16,1280]{6,5,3,1,0,4,2:T(8,128)(2,1)} %convolution_convert_fusion.2), channel_id=1, source_target_pairs={{0,16},{1,17},{2,18},{3,19},{4,20},{5,21},{6,22},{7,23},{8,24},{9,... | collective-permute-start | bytes 3932168 | tf_op jit(solution)/shard_map/ppermute | solution.py:215
  580.3 28.9 %collective-permute-start.29 = (bf16[2,2,2,2,2,16,1280]{6,5,4,2,1,3,0:T(8,128)(2,1)S(1)}, bf16[2,2,2,2,2,16,1280]{6,5,4,2,1,3,0:T(8,128)(2,1)S(1)}, u32[]{:S(2)}, u32[]{:S(2)}) collective-permute-start(bf16[2,2,2,2,2,16,1280]{6,5,4,2,1,3,0:T(8,128)(2,1)S(1)} %copy-done.36), channel_id=1, source_target_pairs={{0,12},{1,13},{2,14},{3,15},{4,8},{5,9},{6,10},{7,11},{8,4},{9,5},... | collective-permute-start | bytes 3932168 | tf_op jit(solution)/shard_map/ppermute | solution.py:215
  586.9 26.9 %collective-permute-start.38 = (bf16[2,2,2,2,2,16,1280]{6,5,3,2,0,1,4:T(8,128)(2,1)S(1)}, bf16[2,2,2,2,2,16,1280]{6,5,3,2,0,1,4:T(8,128)(2,1)S(1)}, u32[]{:S(2)}, u32[]{:S(2)}) collective-permute-start(bf16[2,2,2,2,2,16,1280]{6,5,3,2,0,1,4:T(8,128)(2,1)S(1)} %copy-done.35), channel_id=1, source_target_pairs={{0,4},{1,5},{2,6},{3,7},{4,0},{5,1},{6,2},{7,3},{8,12},{9,13},{10,... | collective-permute-start | bytes 3932168 | tf_op jit(solution)/shard_map/ppermute | solution.py:215
  588.9 29.0 %collective-permute-start.51 = (bf16[2,2,2,2,40,448]{5,4,3,0,1,2:T(8,128)(2,1)S(1)}, bf16[2,2,2,2,40,448]{5,4,3,0,1,2:T(8,128)(2,1)S(1)}, u32[]{:S(2)}, u32[]{:S(2)}) collective-permute-start(bf16[2,2,2,2,40,448]{5,4,3,0,1,2:T(8,128)(2,1)S(1)} %get-tuple-element.50), channel_id=1, source_target_pairs={{0,16},{1,17},{2,18},{3,19},{4,20},{5,21},{6,22},{7,23},{8,24},{9,... | collective-permute-start | bytes 1720328 | tf_op jit(solution)/shard_map/ppermute | solution.py:215
  590.3 27.8 %collective-permute-start.45 = (bf16[2,2,2,2,40,512]{5,4,3,2,1,0:T(8,128)(2,1)S(1)}, bf16[2,2,2,2,40,512]{5,4,3,2,1,0:T(8,128)(2,1)S(1)}, u32[]{:S(2)}, u32[]{:S(2)}) collective-permute-start(bf16[2,2,2,2,40,512]{5,4,3,2,1,0:T(8,128)(2,1)S(1)} %fusion.68), channel_id=1, source_target_pairs={{0,48},{1,49},{2,50},{3,51},{4,52},{5,53},{6,54},{7,55},{8,56},{9,... | collective-permute-start | bytes 1966088 | tf_op jit(solution)/shard_map/ppermute | solution.py:215
  593.8 24.9 %collective-permute-start.27 = (bf16[2,2,2,2,16,1280]{5,4,3,2,1,0:T(8,128)(2,1)S(1)}, bf16[2,2,2,2,16,1280]{5,4,3,2,1,0:T(8,128)(2,1)S(1)}, u32[]{:S(2)}, u32[]{:S(2)}) collective-permute-start(bf16[2,2,2,2,16,1280]{5,4,3,2,1,0:T(8,128)(2,1)S(1)} %fusion.67), channel_id=1, source_target_pairs={{0,12},{1,13},{2,14},{3,15},{4,8},{5,9},{6,10},{7,11},{8,4},{9,5},... | collective-permute-start | bytes 1966088 | tf_op jit(solution)/shard_map/ppermute | solution.py:215
  609.2 18.2 %collective-permute-start.36 = (bf16[2,2,2,2,16,1280]{5,4,2,1,0,3:T(8,128)(2,1)S(1)}, bf16[2,2,2,2,16,1280]{5,4,2,1,0,3:T(8,128)(2,1)S(1)}, u32[]{:S(2)}, u32[]{:S(2)}) collective-permute-start(bf16[2,2,2,2,16,1280]{5,4,2,1,0,3:T(8,128)(2,1)S(1)} %get-tuple-element.56), channel_id=1, source_target_pairs={{0,4},{1,5},{2,6},{3,7},{4,0},{5,1},{6,2},{7,3},{8,12},{9,13},{10,... | collective-permute-start | bytes 1966088 | tf_op jit(solution)/shard_map/ppermute | solution.py:215
  613.8 21.7 %collective-permute-start.30 = (bf16[2,2,2,2,16,1280]{5,4,3,2,1,0:T(8,128)(2,1)S(1)}, bf16[2,2,2,2,16,1280]{5,4,3,2,1,0:T(8,128)(2,1)S(1)}, u32[]{:S(2)}, u32[]{:S(2)}) collective-permute-start(bf16[2,2,2,2,16,1280]{5,4,3,2,1,0:T(8,128)(2,1)S(1)} %get-tuple-element.52), channel_id=1, source_target_pairs={{0,3},{1,2},{2,1},{3,0},{4,7},{5,6},{6,5},{7,4},{8,11},{9,10},{10,... | collective-permute-start | bytes 1966088 | tf_op jit(solution)/shard_map/ppermute | solution.py:215
  617.9 25.8 %collective-permute-start.39 = (bf16[2,2,2,2,16,1280]{5,4,3,2,0,1:T(8,128)(2,1)S(1)}, bf16[2,2,2,2,16,1280]{5,4,3,2,0,1:T(8,128)(2,1)S(1)}, u32[]{:S(2)}, u32[]{:S(2)}) collective-permute-start(bf16[2,2,2,2,16,1280]{5,4,3,2,0,1:T(8,128)(2,1)S(1)} %get-tuple-element.54), channel_id=1, source_target_pairs={{0,1},{1,0},{2,3},{3,2},{4,5},{5,4},{6,7},{7,6},{8,9},{9,8},{10,11... | collective-permute-start | bytes 1966088 | tf_op jit(solution)/shard_map/ppermute | solution.py:215
  618.7 34.8 %collective-permute-start.46 = (bf16[2,2,2,40,512]{4,3,2,1,0:T(8,128)(2,1)S(1)}, bf16[2,2,2,40,512]{4,3,2,1,0:T(8,128)(2,1)S(1)}, u32[]{:S(2)}, u32[]{:S(2)}) collective-permute-start(bf16[2,2,2,40,512]{4,3,2,1,0:T(8,128)(2,1)S(1)} %fusion.126), channel_id=1, source_target_pairs={{0,12},{1,13},{2,14},{3,15},{4,8},{5,9},{6,10},{7,11},{8,4},{9,5},... | collective-permute-start | bytes 983048 | tf_op jit(solution)/shard_map/ppermute | solution.py:215
  625.2 28.5 %collective-permute-start.28 = (bf16[2,2,2,16,1280]{4,3,2,1,0:T(8,128)(2,1)S(1)}, bf16[2,2,2,16,1280]{4,3,2,1,0:T(8,128)(2,1)S(1)}, u32[]{:S(2)}, u32[]{:S(2)}) collective-permute-start(bf16[2,2,2,16,1280]{4,3,2,1,0:T(8,128)(2,1)S(1)} %fusion.123), channel_id=1, source_target_pairs={{0,3},{1,2},{2,1},{3,0},{4,7},{5,6},{6,5},{7,4},{8,11},{9,10},{10,... | collective-permute-start | bytes 983048 | tf_op jit(solution)/shard_map/ppermute | solution.py:215
  634.0 22.1 %collective-permute-start.37 = (bf16[2,2,2,16,1280]{4,3,2,1,0:T(8,128)(2,1)S(1)}, bf16[2,2,2,16,1280]{4,3,2,1,0:T(8,128)(2,1)S(1)}, u32[]{:S(2)}, u32[]{:S(2)}) collective-permute-start(bf16[2,2,2,16,1280]{4,3,2,1,0:T(8,128)(2,1)S(1)} %fusion.117), channel_id=1, source_target_pairs={{0,1},{1,0},{2,3},{3,2},{4,5},{5,4},{6,7},{7,6},{8,9},{9,8},{10,11... | collective-permute-start | bytes 983048 | tf_op jit(solution)/shard_map/ppermute | solution.py:215
  641.2 12.7 %collective-permute-start.31 = (bf16[2,2,2,16,1280]{4,3,2,1,0:T(8,128)(2,1)S(1)}, bf16[2,2,2,16,1280]{4,3,2,1,0:T(8,128)(2,1)S(1)}, u32[]{:S(2)}, u32[]{:S(2)}) collective-permute-start(bf16[2,2,2,16,1280]{4,3,2,1,0:T(8,128)(2,1)S(1)} %fusion.125), channel_id=1, source_target_pairs={{0,48},{1,49},{2,50},{3,51},{4,52},{5,53},{6,54},{7,55},{8,56},{9,... | collective-permute-start | bytes 983048 | tf_op jit(solution)/shard_map/ppermute | solution.py:215
  643.7 9.8 %collective-permute-start.55 = (bf16[40,448]{1,0:T(8,128)(2,1)S(1)}, bf16[40,448]{1,0:T(8,128)(2,1)S(1)}, u32[]{:S(2)}, u32[]{:S(2)}) collective-permute-start(bf16[40,448]{1,0:T(8,128)(2,1)S(1)} %fusion.257), channel_id=1, source_target_pairs={{0,48},{1,49},{2,50},{3,51},{4,52},{5,53},{6,54},{7,55},{8,56},{9,... | collective-permute-start | bytes 107528 | tf_op jit(solution)/shard_map/ppermute | solution.py:215
  654.1 14.9 %collective-permute-start.32 = (bf16[2,2,16,2560]{3,2,1,0:T(8,128)(2,1)S(1)}, bf16[2,2,16,2560]{3,2,1,0:T(8,128)(2,1)S(1)}, u32[]{:S(2)}, u32[]{:S(2)}) collective-permute-start(bf16[2,2,16,2560]{3,2,1,0:T(8,128)(2,1)S(1)} %fusion.130), channel_id=1, source_target_pairs={{0,16},{1,17},{2,18},{3,19},{4,20},{5,21},{6,22},{7,23},{8,24},{9,... | collective-permute-start | bytes 983048 | tf_op jit(solution)/shard_map/ppermute | solution.py:215
  666.0 8.4 %collective-permute-start.41 = (bf16[2,2,16,2560]{3,2,1,0:T(8,128)(2,1)S(1)}, bf16[2,2,16,2560]{3,2,1,0:T(8,128)(2,1)S(1)}, u32[]{:S(2)}, u32[]{:S(2)}) collective-permute-start(bf16[2,2,16,2560]{3,2,1,0:T(8,128)(2,1)S(1)} %fusion.128), channel_id=1, source_target_pairs={{0,48},{1,49},{2,50},{3,51},{4,52},{5,53},{6,54},{7,55},{8,56},{9,... | collective-permute-start | bytes 983048 | tf_op jit(solution)/shard_map/ppermute | solution.py:215
  (147 other events, 2483.8 us)
Sparse Core Ops, SparseCore 0:
  29.8 123.3 all-gather.2
where the time goes:
time: 709 us; the launch traced here: 696 us
  waiting for transfers between devices  268 us (38%)
  local copies, waits for them, and re-layouts  152 us (21%)
  matrix products  147 us (21%)
  starting transfers between devices  66.3 us (9%)
  other arithmetic  45.4 us (6%)
  between operations  17 us (2%)
    ppermute x54, waiting for transfers between devices, halving(): arrived = lax.ppermute(sent, 'dp', partner_pairs(bit))  156 us
    all_gather x1, waiting for transfers between devices, body(): everything = lax.all_gather(packed, 'dp', axis=0, tiled=True)  112 us
    dot_general x41, matrix products, dot(): return jnp.dot(left, right, preferred_element_type=f32)  78.1 us
    ppermute x54, starting transfers between devices, halving(): arrived = lax.ppermute(sent, 'dp', partner_pairs(bit))  62.5 us
    dot_general x25, matrix products, dot_t(): lax.dot_general(left, right, (((1,), (1,)), ((), ())), preferred_element_...  47.5 us
    concatenate x1, local copies, waits for them, and re-layouts, body(): packed = jnp.concatenate(pieces + [w_down[0]], axis=0)[None]  18.6 us
    convert_element_type x39, other arithmetic, halving(): return (next_kept.astype(bf16), next_sent.astype(bf16), left)  17.7 us
  transfers between devices with their start and end apart: 57, of which 30 were waited for; matrix products, arithmetic and copies ran while one was open for 12% of the time, Pallas kernels for 0%

commit v1 on v0

--- a/solution.py
+++ b/solution.py
@@ -288,7 +288,9 @@
     for index, slab in enumerate(slabs):
         pieces += [slab, gain_row if index == 0 else blank]
     packed = jnp.concatenate(pieces + [w_down[0]], axis=0)[None]
-    everything = lax.all_gather(packed, "dp", axis=0, tiled=True)
+    everything = jnp.concatenate(
+        lax.all_to_all(jnp.stack([packed] * lax.axis_size("dp")), "dp", 0, 0), axis=0
+    )
 
     def slab_of(index):
         part = everything[:, PADDED * index : PADDED * (index + 1)]

time: 709 us -> 1080 us (1.52)
  waiting for transfers between devices: 268 us -> 507 us
  local copies, waits for them, and re-layouts: 152 us -> 246 us
  starting transfers between devices: 66.3 us -> 114 us
  between operations: 17 us -> 3.67 us
    all_to_all x0 -> x1, waiting for transfers between devices: none -> 341 us  [body(): lax.all_to_all(jnp.stack([packed] * lax.axis_size('dp')), 'dp', 0, 0)]
    all_gather x1 -> x0, waiting for transfers between devices: 112 us -> none  [body(): everything = lax.all_gather(packed, 'dp', axis=0, tiled=True)]
    slice x1 -> x9, local copies, waits for them, and re-layouts: 11.7 us -> 66 us  [slab_of(): part = everything[:, PADDED * index:PADDED * (index + 1)]]
    all_to_all x0 -> x1, local copies, waits for them, and re-layouts: none -> 43 us  [body(): lax.all_to_all(jnp.stack([packed] * lax.axis_size('dp')), 'dp', 0, 0)]
    ppermute x54, starting transfers between devices: 62.5 us -> 98.8 us  [halving(): arrived = lax.ppermute(sent, 'dp', partner_pairs(bit))]
    concatenate x1, local copies, waits for them, and re-layouts: 18.6 us -> 2.62 us  [body(): packed = jnp.concatenate(pieces + [w_down[0]], axis=0)[None]]
    slice x1 -> x2, local copies, waits for them, and re-layouts: 5.48 us -> 20.3 us  [body(): everything[:, 8 * PADDED:].reshape(FF, D)]
    all_to_all x0 -> x1, starting transfers between devices: none -> 11.9 us  [body(): lax.all_to_all(jnp.stack([packed] * lax.axis_size('dp')), 'dp', 0, 0)]
  transfers between devices with their start and end apart: 57 -> 57, of which waited for: 30 -> 35; matrix products, arithmetic and copies ran while one was open for 12% -> 9% of each run, Pallas kernels for 0% -> 0%
where the time goes in v1:
time: 1080 us; the launch traced here: 1070 us
  waiting for transfers between devices  507 us (47%)
  local copies, waits for them, and re-layouts  246 us (23%)
  matrix products  156 us (14%)
  starting transfers between devices  114 us (11%)
  other arithmetic  40.9 us (4%)
    all_to_all x1, waiting for transfers between devices, body(): lax.all_to_all(jnp.stack([packed] * lax.axis_size('dp')), 'dp', 0, 0)  341 us
    ppermute x54, waiting for transfers between devices, halving(): arrived = lax.ppermute(sent, 'dp', partner_pairs(bit))  166 us
    ppermute x54, starting transfers between devices, halving(): arrived = lax.ppermute(sent, 'dp', partner_pairs(bit))  98.8 us
    dot_general x41, matrix products, dot(): return jnp.dot(left, right, preferred_element_type=f32)  85 us
    slice x9, local copies, waits for them, and re-layouts, slab_of(): part = everything[:, PADDED * index:PADDED * (index + 1)]  66 us
    dot_general x25, matrix products, dot_t(): lax.dot_general(left, right, (((1,), (1,)), ((), ())), preferred_element_...  50.3 us
    all_to_all x1, local copies, waits for them, and re-layouts, body(): lax.all_to_all(jnp.stack([packed] * lax.axis_size('dp')), 'dp', 0, 0)  43 us
  transfers between devices with their start and end apart: 57, of which 35 were waited for; matrix products, arithmetic and copies ran while one was open for 9% of the time, Pallas kernels for 0%

profile of v1, /device:TPU:0, one launch (start us, length us, event | category | flops | bytes accessed | tf_op | source)
XLA Modules:
  0.0 1067.3 jit_solution(8258199018668543564)
XLA Ops:
  7.2 7.6 stack.3
  14.8 11.9 %all-to-all-start = ((bf16[64,1,168,960]{3,2,1,0:T(8,128)(2,1)}), bf16[64,1,168,960]{3,2,1,0:T(8,128)(2,1)}, u32[]{:S(2)}, u32[]{:S(2)}) async-start(bf16[64,1,168,960]{3,2,1,0:T(8,128)(2,1)} %stack.3), calls=%async_computation | async-start | bytes 44040192 | tf_op jit(solution)/shard_map/all_to_all | solution.py:292
  34.9 341.0 %all-to-all-done = bf16[64,1,168,960]{3,2,1,0:T(8,128)(2,1)} async-done(((bf16[64,1,168,960]{3,2,1,0:T(8,128)(2,1)}), bf16[64,1,168,960]{3,2,1,0:T(8,128)(2,1)}, u32[]{:S(2)}, u32[]{:S(2)}) %all-to-all-start) | async-done | bytes 20643872 | tf_op jit(solution)/shard_map/all_to_all | solution.py:292
  375.9 43.0 %copy.258 = bf16[64,1,168,960]{0,3,2,1:T(8,128)(2,1)} copy(bf16[64,1,168,960]{3,2,1,0:T(8,128)(2,1)} %all-to-all-done) | data formatting | bytes 41287680 | tf_op jit(solution)/shard_map/all_to_all | solution.py:292
  419.6 23.8 %fusion.328 = (bf16[64,16,960]{0,2,1:T(8,128)(2,1)}, bf16[64,16,960]{0,2,1:T(8,128)(2,1)}, bf16[64,16,960]{0,2,1:T(8,128)(2,1)}, bf16[64,16,960]{0,2,1:T(8,128)(...) fusion(bf16[64,168,960]{0,2,1:T(8,128)(2,1)} %bitcast.813), kind=kLoop, calls=%fused_computation.648 | loop fusion | bytes 31457280 | tf_op jit(solution)/shard_map/slice | solution.py:296
  459.9 8.2 slice.1024
  500.8 5.7 copy.273
  513.8 5.7 copy.275
  519.4 5.7 copy.276
  525.1 5.6 copy.277
  530.8 5.6 copy.278
  536.4 12.1 %copy.279 = bf16[64,40,960]{2,1,0:T(8,128)(2,1)} copy(bf16[64,40,960]{0,2,1:T(8,128)(2,1)} %slice.1024) | data formatting | bytes 9830400 | tf_op jit(solution)/shard_map/slice | solution.py:308
  551.3 9.2 concatenate.109
  565.1 9.3 concatenate.110
  574.3 7.0 fusion.42
  583.3 5.4 fusion.349
  620.0 5.0 fusion.27
  720.5 26.4 %collective-permute-start.44 = (bf16[2,2,2,2,2,40,512]{6,5,4,3,1,2,0:T(8,128)(2,1)}, bf16[2,2,2,2,2,40,512]{6,5,4,3,1,2,0:T(8,128)(2,1)}, u32[]{:S(2)}, u32[]{:S(2)}) collective-permute-start(bf16[2,2,2,2,2,40,512]{6,5,4,3,1,2,0:T(8,128)(2,1)} %convolution_convert_fusion.10), channel_id=1, source_target_pairs={{0,3},{1,2},{2,1},{3,0},{4,7},{5,6},{6,5},{7,4},{8,11},{9,10},{10,... | collective-permute-start | bytes 3932168 | tf_op jit(solution)/shard_map/ppermute | solution.py:215
  752.1 6.6 collective-permute-start.50
  803.2 15.4 %collective-permute-start.17 = (bf16[2,2,2,2,2,16,320]{6,5,2,3,0,1,4:T(8,128)(2,1)}, bf16[2,2,2,2,2,16,320]{6,5,2,3,0,1,4:T(8,128)(2,1)}, u32[]{:S(2)}, u32[]{:S(2)}) collective-permute-start(bf16[2,2,2,2,2,16,320]{6,5,2,3,0,1,4:T(8,128)(2,1)} %convolution_convert_fusion.18), channel_id=1, source_target_pairs={{0,4},{1,5},{2,6},{3,7},{4,0},{5,1},{6,2},{7,3},{8,12},{9,13},{10,... | collective-permute-start | bytes 983048 | tf_op jit(solution)/shard_map/ppermute | solution.py:215
  832.7 8.1 collective-permute-done.5
  862.0 5.5 collective-permute-done.15
  868.9 5.2 collective-permute-done.7
  879.4 5.9 collective-permute-done.3
  894.5 5.8 collective-permute-done.4
  913.3 5.2 collective-permute-done.24
  923.9 5.5 collective-permute-done.11
  937.8 18.5 %collective-permute-done.13 = bf16[16,1408]{1,0:T(8,128)(2,1)S(1)} collective-permute-done((bf16[16,1408]{1,0:T(8,128)(2,1)S(1)}, bf16[16,1408]{1,0:T(8,128)(2,1)S(1)}, u32[]{:S(2)}, u32[]{:S(2)}) %collective-permute-start.13) | collective-permute-done | bytes 45088 | tf_op jit(solution)/shard_map/ppermute | solution.py:215
  970.2 14.3 %collective-permute-done.35 = bf16[2,2,2,2,2,16,1280]{6,5,3,1,0,4,2:T(8,128)(2,1)S(1)} collective-permute-done((bf16[2,2,2,2,2,16,1280]{6,5,3,1,0,4,2:T(8,128)(2,1)S(1)}, bf16[2,2,2,2,2,16,1280]{6,5,3,1,0,4,2:T(8,128)(2,1)S(1)}, u32[]{:S(2)}, u32[]{:S(2)}) %collective-permute-start.35) | collective-permute-done | bytes 1310752 | tf_op jit(solution)/shard_map/ppermute | solution.py:215
  998.0 8.2 collective-permute-done.52
  1011.5 6.4 collective-permute-done.53
  1021.4 5.7 collective-permute-done.54
  (667 shorter events, 409.2 us)
Async XLA Ops:
  14.8 361.1 %all-to-all-start = ((bf16[64,1,168,960]{3,2,1,0:T(8,128)(2,1)}), bf16[64,1,168,960]{3,2,1,0:T(8,128)(2,1)}, u32[]{:S(2)}, u32[]{:S(2)}) async-start(bf16[64,1,168,960]{3,2,1,0:T(8,128)(2,1)} %stack.3), calls=%async_computation | async-start | bytes 44040192 | tf_op jit(solution)/shard_map/all_to_all | solution.py:292
  720.5 238.1 %collective-permute-start.44 = (bf16[2,2,2,2,2,40,512]{6,5,4,3,1,2,0:T(8,128)(2,1)}, bf16[2,2,2,2,2,40,512]{6,5,4,3,1,2,0:T(8,128)(2,1)}, u32[]{:S(2)}, u32[]{:S(2)}) collective-permute-start(bf16[2,2,2,2,2,40,512]{6,5,4,3,1,2,0:T(8,128)(2,1)} %convolution_convert_fusion.10), channel_id=1, source_target_pairs={{0,3},{1,2},{2,1},{3,0},{4,7},{5,6},{6,5},{7,4},{8,11},{9,10},{10,... | collective-permute-start | bytes 3932168 | tf_op jit(solution)/shard_map/ppermute | solution.py:215
  752.1 182.3 %collective-permute-start.50 = (bf16[2,2,2,2,2,40,448]{6,5,4,0,2,3,1:T(8,128)(2,1)}, bf16[2,2,2,2,2,40,448]{6,5,4,0,2,3,1:T(8,128)(2,1)}, u32[]{:S(2)}, u32[]{:S(2)}) collective-permute-start(bf16[2,2,2,2,2,40,448]{6,5,4,0,2,3,1:T(8,128)(2,1)} %convolution_convert_fusion.8), channel_id=1, source_target_pairs={{0,1},{1,0},{2,3},{3,2},{4,5},{5,4},{6,7},{7,6},{8,9},{9,8},{10,11... | collective-permute-start | bytes 3440648 | tf_op jit(solution)/shard_map/ppermute | solution.py:215
  787.1 65.2 %collective-permute-start.2 = (bf16[2,2,2,2,2,16,512]{6,5,4,2,0,3,1:T(8,128)(2,1)}, bf16[2,2,2,2,2,16,512]{6,5,4,2,0,3,1:T(8,128)(2,1)}, u32[]{:S(2)}, u32[]{:S(2)}) collective-permute-start(bf16[2,2,2,2,2,16,512]{6,5,4,2,0,3,1:T(8,128)(2,1)} %fusion.34), channel_id=1, source_target_pairs={{0,48},{1,49},{2,50},{3,51},{4,52},{5,53},{6,54},{7,55},{8,56},{9,... | collective-permute-start | bytes 1572872 | tf_op jit(solution)/shard_map/ppermute | solution.py:215
  803.2 25.3 %collective-permute-start.17 = (bf16[2,2,2,2,2,16,320]{6,5,2,3,0,1,4:T(8,128)(2,1)}, bf16[2,2,2,2,2,16,320]{6,5,2,3,0,1,4:T(8,128)(2,1)}, u32[]{:S(2)}, u32[]{:S(2)}) collective-permute-start(bf16[2,2,2,2,2,16,320]{6,5,2,3,0,1,4:T(8,128)(2,1)} %convolution_convert_fusion.18), channel_id=1, source_target_pairs={{0,4},{1,5},{2,6},{3,7},{4,0},{5,1},{6,2},{7,3},{8,12},{9,13},{10,... | collective-permute-start | bytes 983048 | tf_op jit(solution)/shard_map/ppermute | solution.py:215
  819.7 11.5 %collective-permute-start.14 = (bf16[2,2,2,2,2,16,384]{6,5,1,3,0,4,2:T(8,128)(2,1)}, bf16[2,2,2,2,2,16,384]{6,5,1,3,0,4,2:T(8,128)(2,1)}, u32[]{:S(2)}, u32[]{:S(2)}) collective-permute-start(bf16[2,2,2,2,2,16,384]{6,5,1,3,0,4,2:T(8,128)(2,1)} %convolution_convert_fusion.20), channel_id=1, source_target_pairs={{0,16},{1,17},{2,18},{3,19},{4,20},{5,21},{6,22},{7,23},{8,24},{9,... | collective-permute-start | bytes 1179656 | tf_op jit(solution)/shard_map/ppermute | solution.py:215
  828.5 12.3 %collective-permute-start.5 = (bf16[2,2,2,2,2,16,384]{6,5,4,2,1,3,0:T(8,128)(2,1)}, bf16[2,2,2,2,2,16,384]{6,5,4,2,1,3,0:T(8,128)(2,1)S(1)}, u32[]{:S(2)}, u32[]{:S(2)}) collective-permute-start(bf16[2,2,2,2,2,16,384]{6,5,4,2,1,3,0:T(8,128)(2,1)} %convolution_convert_fusion.22), channel_id=1, source_target_pairs={{0,12},{1,13},{2,14},{3,15},{4,8},{5,9},{6,10},{7,11},{8,4},{9,5},... | collective-permute-start | bytes 1179656 | tf_op jit(solution)/shard_map/ppermute | solution.py:215
  831.2 13.2 %collective-permute-start.20 = (bf16[2,2,2,2,2,16,448]{6,5,2,4,0,3,1:T(8,128)(2,1)}, bf16[2,2,2,2,2,16,448]{6,5,2,4,0,3,1:T(8,128)(2,1)S(1)}, u32[]{:S(2)}, u32[]{:S(2)}) collective-permute-start(bf16[2,2,2,2,2,16,448]{6,5,2,4,0,3,1:T(8,128)(2,1)} %convolution_convert_fusion.12), channel_id=1, source_target_pairs={{0,1},{1,0},{2,3},{3,2},{4,5},{5,4},{6,7},{7,6},{8,9},{9,8},{10,11... | collective-permute-start | bytes 1376264 | tf_op jit(solution)/shard_map/ppermute | solution.py:215
  840.7 15.5 %collective-permute-start.8 = (bf16[2,2,2,2,2,16,512]{6,5,4,3,1,2,0:T(8,128)(2,1)}, bf16[2,2,2,2,2,16,512]{6,5,4,3,1,2,0:T(8,128)(2,1)S(1)}, u32[]{:S(2)}, u32[]{:S(2)}) collective-permute-start(bf16[2,2,2,2,2,16,512]{6,5,4,3,1,2,0:T(8,128)(2,1)} %convolution_convert_fusion.14), channel_id=1, source_target_pairs={{0,3},{1,2},{2,1},{3,0},{4,7},{5,6},{6,5},{7,4},{8,11},{9,10},{10,... | collective-permute-start | bytes 1572872 | tf_op jit(solution)/shard_map/ppermute | solution.py:215
  850.1 111.6 %collective-permute-start.29 = (bf16[2,2,2,2,2,16,1280]{6,5,4,2,1,3,0:T(8,128)(2,1)}, bf16[2,2,2,2,2,16,1280]{6,5,4,2,1,3,0:T(8,128)(2,1)}, u32[]{:S(2)}, u32[]{:S(2)}) collective-permute-start(bf16[2,2,2,2,2,16,1280]{6,5,4,2,1,3,0:T(8,128)(2,1)} %convolution_convert_fusion.4), channel_id=1, source_target_pairs={{0,12},{1,13},{2,14},{3,15},{4,8},{5,9},{6,10},{7,11},{8,4},{9,5},... | collective-permute-start | bytes 3932168 | tf_op jit(solution)/shard_map/ppermute | solution.py:215
  852.2 9.6 collective-permute-start.6
  867.5 17.8 %collective-permute-start.3 = (bf16[2,2,2,2,16,512]{5,4,3,2,1,0:T(8,128)(2,1)S(1)}, bf16[2,2,2,2,16,512]{5,4,3,2,1,0:T(8,128)(2,1)S(1)}, u32[]{:S(2)}, u32[]{:S(2)}) collective-permute-start(bf16[2,2,2,2,16,512]{5,4,3,2,1,0:T(8,128)(2,1)S(1)} %fusion.147), channel_id=1, source_target_pairs={{0,12},{1,13},{2,14},{3,15},{4,8},{5,9},{6,10},{7,11},{8,4},{9,5},... | collective-permute-start | bytes 786440 | tf_op jit(solution)/shard_map/ppermute | solution.py:215
  878.7 8.1 collective-permute-start.9
  885.2 79.9 %collective-permute-start.26 = (bf16[2,2,2,2,2,16,1280]{6,5,4,2,0,3,1:T(8,128)(2,1)}, bf16[2,2,2,2,2,16,1280]{6,5,4,2,0,3,1:T(8,128)(2,1)}, u32[]{:S(2)}, u32[]{:S(2)}) collective-permute-start(bf16[2,2,2,2,2,16,1280]{6,5,4,2,0,3,1:T(8,128)(2,1)} %convolution_convert_fusion.6), channel_id=1, source_target_pairs={{0,48},{1,49},{2,50},{3,51},{4,52},{5,53},{6,54},{7,55},{8,56},{9,... | collective-permute-start | bytes 3932168 | tf_op jit(solution)/shard_map/ppermute | solution.py:215
  934.0 33.1 %collective-permute-start.38 = (bf16[2,2,2,2,2,16,1280]{6,5,3,2,0,1,4:T(8,128)(2,1)S(1)}, bf16[2,2,2,2,2,16,1280]{6,5,3,2,0,1,4:T(8,128)(2,1)S(1)}, u32[]{:S(2)}, u32[]{:S(2)}) collective-permute-start(bf16[2,2,2,2,2,16,1280]{6,5,3,2,0,1,4:T(8,128)(2,1)S(1)} %copy-done.36), channel_id=1, source_target_pairs={{0,4},{1,5},{2,6},{3,7},{4,0},{5,1},{6,2},{7,3},{8,12},{9,13},{10,... | collective-permute-start | bytes 3932168 | tf_op jit(solution)/shard_map/ppermute | solution.py:215
  934.4 22.0 %collective-permute-start.13 = (bf16[16,1408]{1,0:T(8,128)(2,1)S(1)}, bf16[16,1408]{1,0:T(8,128)(2,1)S(1)}, u32[]{:S(2)}, u32[]{:S(2)}) collective-permute-start(bf16[16,1408]{1,0:T(8,128)(2,1)S(1)} %fusion.253), channel_id=1, source_target_pairs={{0,4},{1,5},{2,6},{3,7},{4,0},{5,1},{6,2},{7,3},{8,12},{9,13},{10,... | collective-permute-start | bytes 135176 | tf_op jit(solution)/shard_map/ppermute | solution.py:215
  956.4 28.1 %collective-permute-start.35 = (bf16[2,2,2,2,2,16,1280]{6,5,3,1,0,4,2:T(8,128)(2,1)S(1)}, bf16[2,2,2,2,2,16,1280]{6,5,3,1,0,4,2:T(8,128)(2,1)S(1)}, u32[]{:S(2)}, u32[]{:S(2)}) collective-permute-start(bf16[2,2,2,2,2,16,1280]{6,5,3,1,0,4,2:T(8,128)(2,1)S(1)} %copy-done.35), channel_id=1, source_target_pairs={{0,16},{1,17},{2,18},{3,19},{4,20},{5,21},{6,22},{7,23},{8,24},{9,... | collective-permute-start | bytes 3932168 | tf_op jit(solution)/shard_map/ppermute | solution.py:215
  958.7 32.8 %collective-permute-start.51 = (bf16[2,2,2,2,40,448]{5,4,3,0,1,2:T(8,128)(2,1)S(1)}, bf16[2,2,2,2,40,448]{5,4,3,0,1,2:T(8,128)(2,1)S(1)}, u32[]{:S(2)}, u32[]{:S(2)}) collective-permute-start(bf16[2,2,2,2,40,448]{5,4,3,0,1,2:T(8,128)(2,1)S(1)} %get-tuple-element.61), channel_id=1, source_target_pairs={{0,16},{1,17},{2,18},{3,19},{4,20},{5,21},{6,22},{7,23},{8,24},{9,... | collective-permute-start | bytes 1720328 | tf_op jit(solution)/shard_map/ppermute | solution.py:215
  961.7 32.4 %collective-permute-start.45 = (bf16[2,2,2,2,40,512]{5,4,3,2,1,0:T(8,128)(2,1)S(1)}, bf16[2,2,2,2,40,512]{5,4,3,2,1,0:T(8,128)(2,1)S(1)}, u32[]{:S(2)}, u32[]{:S(2)}) collective-permute-start(bf16[2,2,2,2,40,512]{5,4,3,2,1,0:T(8,128)(2,1)S(1)} %fusion.68), channel_id=1, source_target_pairs={{0,48},{1,49},{2,50},{3,51},{4,52},{5,53},{6,54},{7,55},{8,56},{9,... | collective-permute-start | bytes 1966088 | tf_op jit(solution)/shard_map/ppermute | solution.py:215
  965.1 29.2 %collective-permute-start.30 = (bf16[2,2,2,2,16,1280]{5,4,3,2,1,0:T(8,128)(2,1)S(1)}, bf16[2,2,2,2,16,1280]{5,4,3,2,1,0:T(8,128)(2,1)S(1)}, u32[]{:S(2)}, u32[]{:S(2)}) collective-permute-start(bf16[2,2,2,2,16,1280]{5,4,3,2,1,0:T(8,128)(2,1)S(1)} %get-tuple-element.63), channel_id=1, source_target_pairs={{0,3},{1,2},{2,1},{3,0},{4,7},{5,6},{6,5},{7,4},{8,11},{9,10},{10,... | collective-permute-start | bytes 1966088 | tf_op jit(solution)/shard_map/ppermute | solution.py:215
  967.1 44.2 %collective-permute-start.27 = (bf16[2,2,2,2,16,1280]{5,4,3,2,1,0:T(8,128)(2,1)S(1)}, bf16[2,2,2,2,16,1280]{5,4,3,2,1,0:T(8,128)(2,1)S(1)}, u32[]{:S(2)}, u32[]{:S(2)}) collective-permute-start(bf16[2,2,2,2,16,1280]{5,4,3,2,1,0:T(8,128)(2,1)S(1)} %fusion.67), channel_id=1, source_target_pairs={{0,12},{1,13},{2,14},{3,15},{4,8},{5,9},{6,10},{7,11},{8,4},{9,5},... | collective-permute-start | bytes 1966088 | tf_op jit(solution)/shard_map/ppermute | solution.py:215
  984.5 34.4 %collective-permute-start.39 = (bf16[2,2,2,2,16,1280]{5,4,3,2,0,1:T(8,128)(2,1)S(1)}, bf16[2,2,2,2,16,1280]{5,4,3,2,0,1:T(8,128)(2,1)S(1)}, u32[]{:S(2)}, u32[]{:S(2)}) collective-permute-start(bf16[2,2,2,2,16,1280]{5,4,3,2,0,1:T(8,128)(2,1)S(1)} %get-tuple-element.65), channel_id=1, source_target_pairs={{0,1},{1,0},{2,3},{3,2},{4,5},{5,4},{6,7},{7,6},{8,9},{9,8},{10,11... | collective-permute-start | bytes 1966088 | tf_op jit(solution)/shard_map/ppermute | solution.py:215
  991.5 35.6 %collective-permute-start.36 = (bf16[2,2,2,2,16,1280]{5,4,2,1,0,3:T(8,128)(2,1)S(1)}, bf16[2,2,2,2,16,1280]{5,4,2,1,0,3:T(8,128)(2,1)S(1)}, u32[]{:S(2)}, u32[]{:S(2)}) collective-permute-start(bf16[2,2,2,2,16,1280]{5,4,2,1,0,3:T(8,128)(2,1)S(1)} %get-tuple-element.67), channel_id=1, source_target_pairs={{0,4},{1,5},{2,6},{3,7},{4,0},{5,1},{6,2},{7,3},{8,12},{9,13},{10,... | collective-permute-start | bytes 1966088 | tf_op jit(solution)/shard_map/ppermute | solution.py:215
  994.1 12.1 %collective-permute-start.52 = (bf16[2,2,2,40,448]{4,3,2,0,1:T(8,128)(2,1)S(1)}, bf16[2,2,2,40,448]{4,3,2,0,1:T(8,128)(2,1)S(1)}, u32[]{:S(2)}, u32[]{:S(2)}) collective-permute-start(bf16[2,2,2,40,448]{4,3,2,0,1:T(8,128)(2,1)S(1)} %fusion.122), channel_id=1, source_target_pairs={{0,4},{1,5},{2,6},{3,7},{4,0},{5,1},{6,2},{7,3},{8,12},{9,13},{10,... | collective-permute-start | bytes 860168 | tf_op jit(solution)/shard_map/ppermute | solution.py:215
  994.3 38.2 %collective-permute-start.46 = (bf16[2,2,2,40,512]{4,3,2,1,0:T(8,128)(2,1)S(1)}, bf16[2,2,2,40,512]{4,3,2,1,0:T(8,128)(2,1)S(1)}, u32[]{:S(2)}, u32[]{:S(2)}) collective-permute-start(bf16[2,2,2,40,512]{4,3,2,1,0:T(8,128)(2,1)S(1)} %fusion.126), channel_id=1, source_target_pairs={{0,12},{1,13},{2,14},{3,15},{4,8},{5,9},{6,10},{7,11},{8,4},{9,5},... | collective-permute-start | bytes 983048 | tf_op jit(solution)/shard_map/ppermute | solution.py:215
  1006.2 27.1 %collective-permute-start.31 = (bf16[2,2,2,16,1280]{4,3,2,1,0:T(8,128)(2,1)S(1)}, bf16[2,2,2,16,1280]{4,3,2,1,0:T(8,128)(2,1)S(1)}, u32[]{:S(2)}, u32[]{:S(2)}) collective-permute-start(bf16[2,2,2,16,1280]{4,3,2,1,0:T(8,128)(2,1)S(1)} %fusion.125), channel_id=1, source_target_pairs={{0,48},{1,49},{2,50},{3,51},{4,52},{5,53},{6,54},{7,55},{8,56},{9,... | collective-permute-start | bytes 983048 | tf_op jit(solution)/shard_map/ppermute | solution.py:215
  1018.0 15.4 %collective-permute-start.28 = (bf16[2,2,2,16,1280]{4,3,2,1,0:T(8,128)(2,1)S(1)}, bf16[2,2,2,16,1280]{4,3,2,1,0:T(8,128)(2,1)S(1)}, u32[]{:S(2)}, u32[]{:S(2)}) collective-permute-start(bf16[2,2,2,16,1280]{4,3,2,1,0:T(8,128)(2,1)S(1)} %fusion.123), channel_id=1, source_target_pairs={{0,3},{1,2},{2,1},{3,0},{4,7},{5,6},{6,5},{7,4},{8,11},{9,10},{10,... | collective-permute-start | bytes 983048 | tf_op jit(solution)/shard_map/ppermute | solution.py:215
  1018.9 8.2 collective-permute-start.54
  1027.1 7.7 collective-permute-start.40
  1032.4 8.9 collective-permute-start.37
  1033.6 15.0 %collective-permute-start.32 = (bf16[2,2,16,2560]{3,2,1,0:T(8,128)(2,1)S(1)}, bf16[2,2,16,2560]{3,2,1,0:T(8,128)(2,1)S(1)}, u32[]{:S(2)}, u32[]{:S(2)}) collective-permute-start(bf16[2,2,16,2560]{3,2,1,0:T(8,128)(2,1)S(1)} %fusion.130), channel_id=1, source_target_pairs={{0,16},{1,17},{2,18},{3,19},{4,20},{5,21},{6,22},{7,23},{8,24},{9,... | collective-permute-start | bytes 983048 | tf_op jit(solution)/shard_map/ppermute | solution.py:215
  1044.3 8.4 collective-permute-start.41
  (163 other events, 2276.0 us)
